TPU v7x, 256 devices: a whole 4x4x8 slice. The times are simulated.
256 devices in a mesh: seq: 64 (over y, z, core), head: 4 (over x).
Axes of the slice: x: 4, y: 4, z: 8, core: 2. Of those that a mesh axis runs over, the one named last changes fastest.
Arguments:
- queries: bfloat16 [32768, 2048], P('seq', 'head'), may hold values from -5 to 5
- keys: bfloat16 [32768, 2048], P('seq', 'head'), may hold values from -5 to 5
- values: bfloat16 [32768, 2048], P('seq', 'head'), may hold values from -5 to 5
- out_weight: bfloat16 [2048, 2048], P('head'), may hold values from -0.125 to 0.125
- out_grad: bfloat16 [32768, 2048], P('seq'), may hold values from -5 to 5
- global_pos: int32 [256], replicated, may hold values from 0 to 511, as said below
- block_mask: int32 [256, 4], P('seq'), may hold values 0 or 1
Outputs:
- layer_out: bfloat16 [32768, 2048], P('seq', 'head')
- grad_queries: bfloat16 [32768, 2048], P('seq', 'head')
- grad_keys: bfloat16 [32768, 2048], P('seq', 'head')
- grad_values: bfloat16 [32768, 2048], P('seq', 'head')
Inputs may be any that keep to these rules, and one draw needn't show every extreme that they name: `global_pos`: 256 distinct positions among the first 512 tokens.
All inputs are finite; a program needn't handle non-finite values. No bound on the sum of `block_mask` on one device may be relied on, other than what follows from the above.
Results may differ from a plain program's by a relative error of at most 0.012.
Values may be sent and summed in bfloat16 or wider, within the bound.
A program may use at most 192 MiB of HBM per device.

v0:
```python
import math

import jax
import jax.numpy as jnp
from jax import lax
from jax.sharding import PartitionSpec as P

HEAD_DIM = 128
BLOCK = 128
WBLK = 4
GLOBALS = 256


def spread(value, axis, source):
    kept = jnp.where(lax.axis_index(axis) == source, value, 0).astype(value.dtype)
    return lax.psum(kept, axis)


def shifted(block, axis, distance):
    devices = range(lax.axis_size(axis))
    route = [(i - distance, i) for i in devices if i - distance in devices]
    return lax.ppermute(block, axis, route)


def split_heads(matrix, head_count):
    return matrix.reshape(matrix.shape[0], head_count, HEAD_DIM)


def window_stack(padded, n_blocks):
    blocks = padded.reshape((n_blocks + WBLK - 1, BLOCK) + padded.shape[1:])
    return jnp.stack(
        [blocks[WBLK - 1 - offset : WBLK - 1 - offset + n_blocks] for offset in range(WBLK)], axis=1
    )


def window_unfold(window_terms, n_blocks):
    summed = jnp.zeros((n_blocks + WBLK - 1,) + window_terms.shape[2:], jnp.float32)
    for offset in range(WBLK):
        summed = summed.at[WBLK - 1 - offset : WBLK - 1 - offset + n_blocks].add(
            window_terms[:, offset]
        )
    return summed.reshape((n_blocks + WBLK - 1) * BLOCK, -1)


def on_device(queries, keys, values, out_weight, out_grad, global_pos, block_mask):
    exact_prec = lax.Precision.HIGHEST
    score_scale = 1.0 / math.sqrt(HEAD_DIM)
    seq_index = lax.axis_index("seq")
    tok_rows = queries.shape[0]
    local_cols = queries.shape[1]
    local_heads = local_cols // HEAD_DIM
    n_blocks = tok_rows // BLOCK
    rim_blocks = WBLK - 1
    rim_rows = rim_blocks * BLOCK
    is_owner = seq_index == 0
    row_index = jnp.arange(tok_rows)
    owner_hits = (row_index[:, None] == global_pos[None, :]) & is_owner
    row_global = jnp.any(owner_hits, axis=1)
    onehot_bf = owner_hits.astype(jnp.bfloat16)
    rim_index = row_index[tok_rows - rim_rows :]
    rim_global = jnp.any(rim_index[:, None] == global_pos[None, :], axis=1) & (seq_index == 1)
    key_global = jnp.concatenate([rim_global, row_global]).astype(jnp.int32)
    d_attn = lax.dot_general(
        out_grad, out_weight, (((1,), (1,)), ((), ())), preferred_element_type=jnp.float32
    ).astype(jnp.bfloat16)
    key_glob, value_glob, query_glob, dattn_glob = (
        spread(jnp.take(keys, global_pos, axis=0), "seq", 0),
        spread(jnp.take(values, global_pos, axis=0), "seq", 0),
        spread(jnp.take(queries, global_pos, axis=0), "seq", 0),
        spread(jnp.take(d_attn, global_pos, axis=0), "seq", 0),
    )
    key_rim, value_rim = shifted(
        (keys[tok_rows - rim_rows :], values[tok_rows - rim_rows :]), "seq", 1
    )
    query_rows = split_heads(query_glob, local_heads)
    key_heads = split_heads(keys, local_heads)
    value_heads = split_heads(values, local_heads)
    key_glob_heads = split_heads(key_glob, local_heads)
    value_glob_heads = split_heads(value_glob, local_heads)
    row_scores = (
        jnp.einsum("ghd,thd->hgt", query_rows, key_heads, preferred_element_type=jnp.float32)
        * score_scale
    )
    value_f32 = value_heads.astype(jnp.float32)
    row_max = lax.pmax(jnp.max(row_scores, axis=2), "seq")
    row_exp = jnp.exp(row_scores - row_max[:, :, None])
    row_total, row_numer = lax.psum(
        (
            jnp.sum(row_exp, axis=2),
            jnp.einsum("hgt,thd->hgd", row_exp, value_f32, precision=exact_prec),
        ),
        "seq",
    )
    row_lse = row_max + jnp.log(row_total)
    row_prob = jnp.exp(row_scores - row_lse[:, :, None])
    attn_rows = (
        (row_numer / row_total[:, :, None])
        .transpose(1, 0, 2)
        .reshape(GLOBALS, local_cols)
        .astype(jnp.bfloat16)
    )
    key_win = window_stack(
        split_heads(jnp.concatenate([key_rim, keys], axis=0), local_heads), n_blocks
    )
    value_win = window_stack(
        split_heads(jnp.concatenate([value_rim, values], axis=0), local_heads), n_blocks
    )
    query_blk = queries.reshape(n_blocks, BLOCK, local_heads, HEAD_DIM)
    block_ids = seq_index * n_blocks + jnp.arange(n_blocks)
    offsets = jnp.arange(WBLK)
    block_ok = (block_ids[:, None] - offsets[None, :] >= 0) & (block_mask == 1)
    causal_ok = (offsets[None, None, :, None] > 0) | (
        jnp.arange(BLOCK)[None, None, None, :] <= jnp.arange(BLOCK)[None, :, None, None]
    )
    key_glob_win = window_stack(key_global, n_blocks)
    pair_ok = block_ok[:, None, :, None] & causal_ok & (key_glob_win[:, None] == 0)
    win_scores = (
        jnp.einsum("bihd,brjhd->hbirj", query_blk, key_win, preferred_element_type=jnp.float32)
        * score_scale
    )
    win_scores = jnp.where(pair_ok[None], win_scores, -jnp.inf)
    glob_scores = (
        jnp.einsum("bihd,ghd->hbig", query_blk, key_glob_heads, preferred_element_type=jnp.float32)
        * score_scale
    )
    row_peak = jnp.maximum(jnp.max(win_scores, axis=(3, 4)), jnp.max(glob_scores, axis=3))
    row_mass = jnp.sum(jnp.exp(win_scores - row_peak[..., None, None]), axis=(3, 4)) + jnp.sum(
        jnp.exp(glob_scores - row_peak[..., None]), axis=3
    )
    win_lse = row_peak + jnp.log(row_mass)
    win_prob = jnp.exp(win_scores - win_lse[..., None, None])
    glob_prob = jnp.exp(glob_scores - win_lse[..., None])
    win_weight = win_prob.astype(jnp.bfloat16)
    glob_weight = glob_prob.astype(jnp.bfloat16)
    attn_win = jnp.einsum(
        "hbirj,brjhd->bihd", win_weight, value_win, preferred_element_type=jnp.float32
    ) + jnp.einsum(
        "hbig,ghd->bihd", glob_weight, value_glob_heads, preferred_element_type=jnp.float32
    )
    attn_from_rows = jnp.dot(onehot_bf, attn_rows, preferred_element_type=jnp.float32)
    attn_local = jnp.where(
        row_global[:, None], attn_from_rows, attn_win.reshape(tok_rows, local_cols)
    ).astype(jnp.bfloat16)
    layer_out = (
        lax.psum_scatter(
            lax.dot_general(
                out_weight, attn_local, (((0,), (1,)), ((), ())), preferred_element_type=jnp.float32
            ).astype(jnp.bfloat16),
            "head",
            scatter_dimension=0,
            tiled=True,
        )
        .astype(jnp.float32)
        .T.astype(jnp.bfloat16)
    )
    dattn_win = jnp.where(row_global[:, None], jnp.zeros_like(d_attn), d_attn)
    delta_win = (
        (dattn_win.astype(jnp.float32) * attn_local.astype(jnp.float32))
        .reshape(tok_rows, local_heads, HEAD_DIM)
        .sum(axis=2)
        .T.reshape(local_heads, n_blocks, BLOCK)
    )
    dattn_blk = dattn_win.reshape(n_blocks, BLOCK, local_heads, HEAD_DIM)
    win_dprob = jnp.einsum(
        "bihd,brjhd->hbirj", dattn_blk, value_win, preferred_element_type=jnp.float32
    )
    glob_dprob = jnp.einsum(
        "bihd,ghd->hbig", dattn_blk, value_glob_heads, preferred_element_type=jnp.float32
    )
    win_dscore = (win_prob * (win_dprob - delta_win[..., None, None])).astype(jnp.bfloat16)
    glob_dscore = (glob_prob * (glob_dprob - delta_win[..., None])).astype(jnp.bfloat16)
    dq_local = jnp.einsum(
        "hbirj,brjhd->bihd", win_dscore, key_win, preferred_element_type=jnp.float32
    ) + jnp.einsum(
        "hbig,ghd->bihd", glob_dscore, key_glob_heads, preferred_element_type=jnp.float32
    )
    dq_local = dq_local.reshape(tok_rows, local_cols)
    dk_win = window_unfold(
        jnp.einsum("hbirj,bihd->brjhd", win_dscore, query_blk, preferred_element_type=jnp.float32),
        n_blocks,
    )
    dv_win = window_unfold(
        jnp.einsum("hbirj,bihd->brjhd", win_weight, dattn_blk, preferred_element_type=jnp.float32),
        n_blocks,
    )
    dk_glob_part = jnp.einsum(
        "hbig,bihd->ghd", glob_dscore, query_blk, preferred_element_type=jnp.float32
    )
    dv_glob_part = jnp.einsum(
        "hbig,bihd->ghd", glob_weight, dattn_blk, preferred_element_type=jnp.float32
    )
    dattn_rows = split_heads(dattn_glob, local_heads)
    delta_rows = (
        (dattn_glob.astype(jnp.float32) * attn_rows.astype(jnp.float32))
        .reshape(GLOBALS, local_heads, HEAD_DIM)
        .sum(axis=2)
        .T
    )
    row_dprob = jnp.einsum(
        "ghd,thd->hgt", dattn_rows, value_heads, preferred_element_type=jnp.float32
    )
    row_dscore = (row_prob * (row_dprob - delta_rows[..., None])).astype(jnp.bfloat16)
    row_weight = row_prob.astype(jnp.bfloat16)
    dq_rows_part = jnp.einsum(
        "hgt,thd->ghd", row_dscore, key_heads, preferred_element_type=jnp.float32
    )
    dk_rows = jnp.einsum(
        "hgt,ghd->thd", row_dscore, query_rows, preferred_element_type=jnp.float32
    ).reshape(tok_rows, local_cols)
    dv_rows = jnp.einsum(
        "hgt,ghd->thd", row_weight, dattn_rows, preferred_element_type=jnp.float32
    ).reshape(tok_rows, local_cols)
    dq_sum, dk_sum, dv_sum = lax.psum((dq_rows_part, dk_glob_part, dv_glob_part), "seq")
    dk_back, dv_back = (
        shifted(dk_win[:rim_rows].astype(jnp.bfloat16), "seq", -1).astype(jnp.float32),
        shifted(dv_win[:rim_rows].astype(jnp.bfloat16), "seq", -1).astype(jnp.float32),
    )
    dk_local = dk_win[rim_rows:].at[tok_rows - rim_rows :].add(dk_back)
    dv_local = dv_win[rim_rows:].at[tok_rows - rim_rows :].add(dv_back)

    def owner_rows(summed):
        placed = (
            jnp.zeros((tok_rows, local_cols), jnp.float32)
            .at[global_pos]
            .add(summed.reshape(GLOBALS, local_cols))
        )
        return jnp.where(is_owner, placed, jnp.zeros_like(placed))

    grad_keys = ((dk_local + owner_rows(dk_sum) + dk_rows) * score_scale).astype(jnp.bfloat16)
    grad_values = (dv_local + owner_rows(dv_sum) + dv_rows).astype(jnp.bfloat16)
    grad_queries = ((dq_local + owner_rows(dq_sum)) * score_scale).astype(jnp.bfloat16)
    return (layer_out, grad_queries, grad_keys, grad_values)


def solution(mesh):
    return jax.shard_map(
        on_device,
        mesh=mesh,
        in_specs=(
            P("seq", "head"),
            P("seq", "head"),
            P("seq", "head"),
            P("head", None),
            P("seq", None),
            P(),
            P("seq", None),
        ),
        out_specs=(P("seq", "head"), P("seq", "head"), P("seq", "head"), P("seq", "head")),
        check_vma=False,
    )
```

profile of v0, /device:TPU:2, one launch (start us, length us, event | category | flops | bytes accessed | tf_op | source)
XLA Modules:
  0.0 817.1 jit_solution(5766779199065816381)
XLA Ops:
  9.2 2.5 collective-permute-start
  13.5 4.1 collective-permute-start.1
  22.0 3.7 convolution_convert_fusion.1
  25.7 2.0 copy.218
  27.7 3.0 gather_fusion.3
  30.7 3.0 gather_fusion
  33.8 2.3 select_select_fusion
  46.8 2.0 copy.191
  49.1 2.1 copy.235
  51.9 2.0 copy_dynamic-update-slice_fusion.3
  74.1 4.6 fusion.2
  78.6 151.8 %all-reduce.12.cloned.1.call-done = (bf16[256,4,128]{2,0,1:T(8,128)(2,1)}, bf16[256,4,128]{2,0,1:T(8,128)(2,1)}, bf16[256,4,128]{0,2,1:T(8,128)(2,1)}, bf16[256,512]{1,0:T(8,128)(2,1)}) async-done(((bf16[256,4,128]{2,0,1:T(8,128)(2,1)}, bf16[256,4,128]{2,0,1:T(8,128)(2,1)}, bf16[256,4,128]{0,2,1:T(8,128)(2,1)}, bf16[256,512]{1,0:T(8,128)(2,1)}), (bf16[256,4,128]{2,0,1:T(8,128)(2,1)}, ...) | async-done | bytes 1048592 | tf_op jit(solution)/shard_map/psum | solution.py:16
  230.4 2.7 fusion.82
  233.2 126.0 %pmax.7 = f32[4,256]{1,0:T(4,128)S(1)} all-reduce(f32[4,256]{1,0:T(4,128)S(1)} %get-tuple-element.148), channel_id=1, replica_groups=mesh['seq'=64,'head'=4] {'seq'}, use_global_device_ids=true, to_apply=%region_3.5 | all-reduce | flops 1024 | bytes 8192 | tf_op jit(solution)/shard_map/pmax | solution.py:85
  359.1 3.8 fusion.10
  362.9 2.2 fusion.9
  372.7 124.1 %psum.65 = f32[4,256]{1,0:T(4,128)S(1)} all-reduce(f32[4,256]{1,0:T(4,128)S(1)} %fusion.9), channel_id=1, replica_groups=mesh['seq'=64,'head'=4] {'seq'}, use_global_device_ids=true, to_apply=%region_6.8 | all-reduce | flops 1024 | bytes 8192 | tf_op jit(solution)/shard_map/psum | solution.py:87
  497.0 3.2 fusion.29
  500.2 2.6 copy.250
  502.8 47.1 %all-reduce.8.cloned.1.call-done = f32[4,256,128]{2,1,0:T(8,128)} async-done(((f32[4,256,128]{2,1,0:T(8,128)}), f32[4,256,128]{2,1,0:T(8,128)}) %all-reduce.8.cloned.1.call-update) | async-done | bytes 524304 | tf_op jit(solution)/shard_map/psum | solution.py:87
  552.1 2.6 bitcast_reduce_fusion.1
  555.9 3.2 fusion.68
  559.1 2.7 multiply_convert_fusion.2
  561.9 4.7 multiply_convert_fusion
  569.1 2.3 multiply_convert_fusion.1
  572.3 2.4 fusion.83
  574.7 2.0 copy.225
  576.8 2.3 fusion.84
  583.1 2.4 convolution_bitcast_fusion.1
  588.0 2.3 fusion.42
  590.5 2.7 fusion.40
  595.9 2.3 slice.444
  598.2 2.2 slice.445
  601.5 9.5 %collective-permute-start.2 = (bf16[384,512]{1,0:T(8,128)(2,1)}, bf16[384,512]{1,0:T(8,128)(2,1)}, u32[]{:S(2)}, u32[]{:S(2)}) collective-permute-start(bf16[384,512]{1,0:T(8,128)(2,1)} %bitcast.242), channel_id=1, source_target_pairs={{4,0},{8,4},{12,8},{16,12},{20,16},{24,20},{28,24},{32,28},{36,32}... | collective-permute-start | bytes 1179656 | tf_op jit(solution)/shard_map/ppermute | solution.py:22
  611.0 2.6 fusion.1
  614.6 3.7 convolution_bitcast_fusion
  625.9 3.0 fusion.21
  633.8 2.6 copy.217
  636.4 2.5 copy.238
  643.4 2.3 copy.365
  645.8 2.3 copy.245
  651.5 126.0 %all-reduce.10.cloned.1.call-done = (f32[256,512]{1,0:T(8,128)}, f32[256,512]{1,0:T(8,128)}, f32[256,512]{1,0:T(8,128)}) async-done(((f32[256,512]{1,0:T(8,128)}, f32[256,512]{1,0:T(8,128)}, f32[256,512]{1,0:T(8,128)}), (f32[256,512]{1,0:T(8,128)}, f32[256,512]{1,0:T(8,128)}, f32[256,512]{1,0:T(8,128)})) %all-reduce.10.cloned.1.call-update) | async-done | bytes 1572880 | tf_op jit(solution)/shard_map/psum | solution.py:213
  777.5 3.6 scatter_custom_fusion
  781.1 3.8 scatter_custom_fusion.1
  784.9 3.6 scatter_custom_fusion.2
  788.5 2.4 fusion.32
  791.0 2.6 multiply_convert_fusion.3
  794.8 15.6 %reduce-scatter.2.cloned.1.call-done = bf16[512,512]{0,1:T(8,128)(2,1)} async-done(((bf16[2048,512]{0,1:T(8,128)(2,1)}), bf16[512,512]{0,1:T(8,128)(2,1)}) %reduce-scatter.2.cloned.1.call-update) | async-done | bytes 524304 | tf_op jit(solution)/shard_map/reduce_scatter | solution.py:145
  (205 shorter events, 87.3 us)
Async XLA Ops:
  7.2 14.8 %copy-start = (bf16[512,2048]{1,0:T(8,128)(2,1)S(1)}, bf16[512,2048]{1,0:T(8,128)(2,1)}, u32[]{:S(2)}) copy-start(bf16[512,2048]{1,0:T(8,128)(2,1)} %param.32) | copy-start | bytes 6291460
  7.2 13.0 %copy-start.3 = (bf16[512,512]{1,0:T(8,128)(2,1)S(1)}, bf16[512,512]{1,0:T(8,128)(2,1)}, u32[]{:S(2)}) copy-start(bf16[512,512]{1,0:T(8,128)(2,1)} %param.31) | copy-start | bytes 1572868
  7.2 11.8 %copy-start.4 = (bf16[512,512]{1,0:T(8,128)(2,1)S(1)}, bf16[512,512]{1,0:T(8,128)(2,1)}, u32[]{:S(2)}) copy-start(bf16[512,512]{1,0:T(8,128)(2,1)} %param.30) | copy-start | bytes 1572868
  7.2 223.2 %all-reduce.12.cloned.1.call-start = ((), (), s32[]{:S(2)}) async-start(), calls=%async_computation.4 | async-start | bytes 2097152 | tf_op jit(solution)/shard_map/psum | solution.py:16
  9.2 44.8 %collective-permute-start = (bf16[384,512]{1,0:T(8,128)(2,1)}, bf16[384,512]{1,0:T(8,128)(2,1)}, u32[]{:S(2)}, u32[]{:S(2)}) collective-permute-start(bf16[384,512]{1,0:T(8,128)(2,1)} %slice.385), channel_id=1, source_target_pairs={{0,4},{4,8},{8,12},{12,16},{16,20},{20,24},{24,28},{28,32},{32,36}... | collective-permute-start | bytes 1179656 | tf_op jit(solution)/shard_map/ppermute | solution.py:22
  13.5 42.7 %collective-permute-start.1 = (bf16[384,512]{1,0:T(8,128)(2,1)}, bf16[384,512]{1,0:T(8,128)(2,1)}, u32[]{:S(2)}, u32[]{:S(2)}) collective-permute-start(bf16[384,512]{1,0:T(8,128)(2,1)} %slice.398), channel_id=1, source_target_pairs={{0,4},{4,8},{8,12},{12,16},{16,20},{20,24},{24,28},{28,32},{32,36}... | collective-permute-start | bytes 1179656 | tf_op jit(solution)/shard_map/ppermute | solution.py:22
  36.0 5.7 copy-start.45
  41.7 508.1 %all-reduce.8.cloned.1.call-start = ((), (), s32[]{:S(2)}) async-start(), calls=%async_computation.1 | async-start | bytes 1048576 | tf_op jit(solution)/shard_map/psum | solution.py:87
  43.8 7.6 copy-start.46
  51.9 316.0 %copy-start.30 = (pred[4,128,4,128]{1,3,2,0:T(8,128)(4,1)}, pred[4,128,4,128]{1,3,2,0:T(8,128)(4,1)S(1)}, u32[]{:S(2)}) copy-start(pred[4,128,4,128]{1,3,2,0:T(8,128)(4,1)S(1)} %and_and_fusion) | copy-start | bytes 786436
  63.7 2.9 copy-start.33
  74.1 156.4 %copy-start.16 = (bf16[512,512]{0,1:T(8,128)(2,1)S(1)}, bf16[512,512]{0,1:T(8,128)(2,1)}, u32[]{:S(2)}) copy-start(bf16[512,512]{0,1:T(8,128)(2,1)} %copy.299) | copy-start | bytes 1572868
  359.1 6.0 copy-start.17
  362.9 3.7 copy-start.8
  366.6 4.3 copy-start.1
  367.5 1.5 copy-start.44
  369.0 1.8 copy-start.39
  370.9 126.0 %copy-start.34 = (bf16[256,512]{1,0:T(8,128)(2,1)S(1)}, bf16[256,512]{1,0:T(8,128)(2,1)}, u32[]{:S(2)}) copy-start(bf16[256,512]{1,0:T(8,128)(2,1)} %get-tuple-element.131) | copy-start | bytes 786436
  372.7 404.8 %all-reduce.10.cloned.1.call-start = ((), (), s32[]{:S(2)}) async-start(), calls=%async_computation.3 | async-start | bytes 3145728 | tf_op jit(solution)/shard_map/psum | solution.py:213
  555.9 6.0 copy-start.13
  555.9 3.2 copy-start.2
  555.9 5.9 copy-start.9
  559.1 2.8 copy-start.31
  559.1 2.8 copy-start.41
  561.9 4.7 copy-start.35
  561.9 4.7 copy-start.36
  572.3 4.4 copy-start.10
  585.5 2.5 copy-start.7
  590.4 220.0 %reduce-scatter.2.cloned.1.call-start = ((), (), s32[]{:S(2)}) async-start(), calls=%async_computation.2 | async-start | bytes 2621440 | tf_op jit(solution)/shard_map/reduce_scatter | solution.py:145
  598.2 12.8 %copy-start.47 = (bf16[512,512]{0,1:T(8,128)(2,1)S(1)}, bf16[512,512]{0,1:T(8,128)(2,1)}, u32[]{:S(2)}) copy-start(bf16[512,512]{0,1:T(8,128)(2,1)} %get-tuple-element.154) | copy-start | bytes 1572868
  601.5 46.6 %collective-permute-start.2 = (bf16[384,512]{1,0:T(8,128)(2,1)}, bf16[384,512]{1,0:T(8,128)(2,1)}, u32[]{:S(2)}, u32[]{:S(2)}) collective-permute-start(bf16[384,512]{1,0:T(8,128)(2,1)} %bitcast.242), channel_id=1, source_target_pairs={{4,0},{8,4},{12,8},{16,12},{20,16},{24,20},{28,24},{32,28},{36,32}... | collective-permute-start | bytes 1179656 | tf_op jit(solution)/shard_map/ppermute | solution.py:22
  624.5 4.5 copy-start.38
  624.5 25.1 %collective-permute-start.3 = (bf16[384,512]{1,0:T(8,128)(2,1)}, bf16[384,512]{1,0:T(8,128)(2,1)S(1)}, u32[]{:S(2)}, u32[]{:S(2)}) collective-permute-start(bf16[384,512]{1,0:T(8,128)(2,1)} %bitcast.241), channel_id=1, source_target_pairs={{4,0},{8,4},{12,8},{16,12},{20,16},{24,20},{28,24},{32,28},{36,32}... | collective-permute-start | bytes 1179656 | tf_op jit(solution)/shard_map/ppermute | solution.py:22
  625.9 4.4 copy-start.37
  628.9 1.4 copy-start.12
  628.9 2.7 copy-start.6
  628.9 2.7 copy-start.15
  633.8 5.2 copy-start.18
  638.9 1.7 copy-start.28
  639.6 2.5 copy-start.20
  643.4 4.7 copy-start.24
  648.1 2.4 copy-start.29
  650.5 138.0 %copy-start.19 = (f32[4,128,4,128]{3,2,1,0:T(4,128)S(1)}, f32[4,128,4,128]{3,2,1,0:T(4,128)}, u32[]{:S(2)}) copy-start(f32[4,128,4,128]{3,2,1,0:T(4,128)} %copy.217) | copy-start | bytes 3145732
  788.5 2.4 copy-start.22
  788.5 2.4 copy-start.26
  790.9 2.6 copy-start.21
  791.0 2.6 copy-start.23
  791.0 2.6 copy-start.27
  (8 other events, 8.8 us)
Sparse Core Ops, SparseCore 0:
  41.8 188.5 all-reduce.11
  372.8 176.9 all-reduce.7
  590.5 186.9 all-reduce.9
  780.5 29.8 reduce-scatter.1
where the time goes:
time: 829 us; the launch traced here: 817 us
  waiting for transfers between devices  341 us (41%)
  blocking collectives  250 us (30%)
  local copies, waits for them, and re-layouts  99.9 us (12%)
  matrix products  56.3 us (7%)
  other arithmetic  38 us (5%)
  starting transfers between devices  17.6 us (2%)
  between operations  14.7 us (2%)
    psum x1, waiting for transfers between devices, spread(): return lax.psum(kept, axis)  152 us
    psum x1, waiting for transfers between devices, on_device(): lax.psum((dq_rows_part, dk_glob_part, dv_glob_part), 'seq')  126 us
    pmax x1, blocking collectives, on_device(): row_max = lax.pmax(jnp.max(row_scores, axis=2), 'seq')  126 us
    psum x1, blocking collectives, on_device(): lax.psum((jnp.sum(row_exp, axis=2), jnp.einsum('hgt,thd->hgd', row_exp, v...  124 us
    psum x1, waiting for transfers between devices, on_device(): lax.psum((jnp.sum(row_exp, axis=2), jnp.einsum('hgt,thd->hgd', row_exp, v...  47.1 us
    unnamed x105, local copies, waits for them, and re-layouts  19.1 us
    ppermute x4, starting transfers between devices, shifted(): return lax.ppermute(block, axis, route)  17.5 us
  transfers between devices with their start and end apart: 8, of which 4 were waited for; matrix products, arithmetic and copies ran while one was open for 16% of the time, Pallas kernels for 0%

commit v1 on v0

v1 whole, which is shorter than its diff:
```python
import math

import jax
import jax.numpy as jnp
from jax import lax
from jax.experimental import pallas as pl
from jax.experimental.pallas import tpu as pltpu
from jax.sharding import PartitionSpec as P

HD = 128
BLK = 128
WBLK = 4
GLB = 256
TOK = 512
COLS = 512
LH = 4
NB = 4
RIM = 384
D = 2048
NY = 4
NZ = 8
NS = 64
NX = 4
NCH = 16
SCALE = 1.0 / math.sqrt(HD)
NEG = -1e30
F32 = jnp.float32
BF = jnp.bfloat16
MESH = pl.DeviceIdType.MESH


def mm(a, b):
    return lax.dot_general(a, b, (((1,), (0,)), ((), ())), preferred_element_type=F32)


def mm_t(a, b):
    return lax.dot_general(a, b, (((1,), (1,)), ((), ())), preferred_element_type=F32)


def flag(cond):
    return jnp.where(cond, 1, 0).astype(jnp.int32)


def kernel(
    q_hbm, k_hbm, v_hbm, w_hbm, og_hbm, gpos, bmask,
    lo_out, gq_out, gk_out, gv_out,
    q_s, kc, vc, w_s, og_s, da_s, oh_s, gbuf, bias,
    ew, dpw, mw, lw, cw, uw, pg_s, attn_s,
    lp, lr, dkc, dvc, dqa, dkg, dvg, hbs, hbr,
    st1, st2, st3, srt, dpt,
    rb, sib, comb, rs, sl, ogat, rt,
    ld_sem, bs_send, bs_recv, halo_send, halo_recv, hb_send_sem, hb_recv_sem,
    lx_send, lx_recv, s1_send, s1_recv, s2_send, s2_recv, s3_send, s3_recv,
    sib_send, sib_recv, rs_send, rs_recv, og_send, og_recv,
):
    s = lax.axis_index("seq")
    x = lax.axis_index("head")
    core = s % 2
    chip = s // 2
    z = chip % NZ
    y = chip // NZ
    owner = s == 0
    mate = s + 1 - 2 * core

    def seq_of(yy, zz, cc):
        return (yy * NZ + zz) * 2 + cc

    def remote(src, dst, ssem, rsem, to_seq):
        return pltpu.make_async_remote_copy(
            src_ref=src, dst_ref=dst, send_sem=ssem, recv_sem=rsem,
            device_id={"seq": to_seq}, device_id_type=MESH)

    loads = [
        pltpu.make_async_copy(k_hbm, kc.at[pl.ds(RIM, TOK)], ld_sem.at[0]),
        pltpu.make_async_copy(v_hbm, vc.at[pl.ds(RIM, TOK)], ld_sem.at[1]),
        pltpu.make_async_copy(q_hbm, q_s, ld_sem.at[2]),
        pltpu.make_async_copy(og_hbm, og_s, ld_sem.at[3]),
        pltpu.make_async_copy(w_hbm, w_s, ld_sem.at[4]),
    ]
    for copy in loads:
        copy.start()
    for copy in loads[:3]:
        copy.wait()

    nxt = jnp.minimum(s + 1, NS - 1)
    prv = jnp.maximum(s - 1, 0)
    halo = [
        remote(buf.at[pl.ds(RIM + BLK, RIM)], buf.at[pl.ds(0, RIM)], halo_send.at[i], halo_recv.at[i], nxt)
        for i, buf in enumerate((kc, vc))
    ]

    @pl.when(s < NS - 1)
    def _():
        for copy in halo:
            copy.start()

    @pl.when(owner)
    def _():
        kc[pl.ds(0, RIM), :] = jnp.zeros((RIM, COLS), BF)
        vc[pl.ds(0, RIM), :] = jnp.zeros((RIM, COLS), BF)

    hits = jnp.where(
        lax.broadcasted_iota(jnp.int32, (TOK, GLB), 0) == gpos[...], 1.0, 0.0).astype(F32)
    is_row = jnp.max(hits.T, axis=0, keepdims=True)
    own_f = jnp.where(owner, 1.0, 0.0).astype(F32)
    one_f = jnp.where(s == 1, 1.0, 0.0).astype(F32)
    oh_s[...] = (hits * own_f).astype(BF)

    def tree(a, na, b, nb):
        ap = flag(b == 0) * flag(a < na // 2)
        am = flag(b == 0) * (flag(a == 0) + flag(a > na // 2 + 1)) + flag(b != 0) * flag(a == 1)
        bp = flag(a != 0) * flag(b < nb // 2)
        bm = flag(a != 0) * (flag(b == 0) + flag(b > nb // 2 + 1))
        return ap, am, bp, bm

    zp0, zm0, yp0, ym0 = tree(z, NZ, y, NY)
    yp1, ym1, zp1, zm1 = tree(y, NY, z, NZ)
    dirs = (
        (zp0, zp1, seq_of(y, (z + 1) % NZ, 0)),
        (zm0, zm1, seq_of(y, (z + NZ - 1) % NZ, 0)),
        (yp0, yp1, seq_of((y + 1) % NY, z, 0)),
        (ym0, ym1, seq_of((y + NY - 1) % NY, z, 0)),
    )

    def chunk(c):
        start = pl.multiple_of(((c // 2) % 2) * 128, 128)
        return gbuf.at[(c // 4) * 2 + c % 2, pl.ds(start, 128), :]

    def chunk_sends(c, act):
        half = c % 2
        for d, (c0, c1, dev) in enumerate(dirs):
            @pl.when((c0 * (1 - half) + c1 * half) * (1 - core) > 0)
            def _():
                act(remote(chunk(c), chunk(c), bs_send.at[c, d], bs_recv.at[c], dev))

        @pl.when(core == 0)
        def _():
            act(remote(chunk(c), chunk(c), bs_send.at[c, 4], bs_recv.at[c], mate))

    def gather(slot, src):
        got = mm(oh_s[...].astype(F32).T.astype(BF), src).astype(BF)
        gbuf[slot * 2, :, :] = got[:, :256]
        gbuf[slot * 2 + 1, :, :] = got[:, 256:]

    def send_chunks(first):
        @pl.loop(first, first + 8)
        def _(c):
            chunk_sends(c, lambda copy: copy.start())

    @pl.when(owner)
    def _():
        gather(0, q_s[...])
        gather(1, kc[pl.ds(RIM, TOK), :])
        send_chunks(0)

    for copy in loads[3:]:
        copy.wait()

    @pl.loop(0, NB)
    def _(b):
        rows = pl.ds(pl.multiple_of(b * BLK, BLK), BLK)
        da_s[rows, :] = mm_t(og_s[rows, :], w_s[...]).astype(BF)

    @pl.when(owner)
    def _():
        gather(2, da_s[...])
        gather(3, vc[pl.ds(RIM, TOK), :])
        send_chunks(8)
        is_col = jnp.max(oh_s[...].astype(F32), axis=1, keepdims=True)
        da_s[...] = jnp.where(is_col > 0, 0.0, da_s[...].astype(F32)).astype(BF)

    f_rim = is_row[:, 128:512] * one_f
    f_loc = is_row * own_f
    ii = lax.broadcasted_iota(jnp.int32, (BLK, BLK), 0)
    jj = lax.broadcasted_iota(jnp.int32, (BLK, BLK), 1)
    causal = jnp.where(jj <= ii, 0.0, NEG)
    for b in range(NB):
        for part in range(WBLK):
            r = WBLK - 1 - part
            ok = flag(bmask[b, r] == 1) * flag(s * NB + b - r >= 0)
            base = jnp.where(ok == 1, 0.0, NEG).astype(F32)
            at = b + part
            tok = f_rim[:, at * 128:(at + 1) * 128] if at < 3 else f_loc[:, (at - 3) * 128:(at - 2) * 128]
            tile = jnp.broadcast_to(tok * NEG + base, (BLK, BLK))
            if r == 0:
                tile = tile + causal
            bias[b, :, part * 128:(part + 1) * 128] = tile

    dkc[...] = jnp.zeros(dkc.shape, F32)
    dvc[...] = jnp.zeros(dvc.shape, F32)
    dkg[...] = jnp.zeros(dkg.shape, F32)
    dvg[...] = jnp.zeros(dvg.shape, F32)

    def spans(b, h):
        row0 = pl.multiple_of(b * BLK, BLK)
        return pl.ds(row0, BLK), pl.ds(row0, WBLK * BLK), pl.ds(pl.multiple_of(h * HD, HD), HD)

    def window_unit(u):
        b = NB - 1 - u // LH
        h = u % LH
        rows, win, cols = spans(b, h)
        sc = mm_t(q_s[rows, cols], kc[win, cols]) * SCALE + bias[b]
        top = jnp.max(sc, axis=1, keepdims=True)
        ex = jnp.exp(sc - top)
        i = b * LH + h
        ew[i] = ex
        mw[i] = top
        lw[i] = jnp.sum(ex, axis=1, keepdims=True)
        uw[rows, cols] = mm(ex.astype(BF), vc[win, cols])
        dpw[i] = mm_t(da_s[rows, cols], vc[win, cols])

    dz = jnp.minimum(z, NZ - z)
    dy = jnp.minimum(y, NY - y)
    depth = dz + dy
    leaf = flag(depth > 5) + core
    late_units = jnp.where(leaf > 0, 0, jnp.maximum(16 - 4 * depth, 0))
    late_relay = jnp.where(leaf > 0, 16, jnp.where(depth == 5, 4, 0))

    @pl.loop(0, 32)
    def _(t):
        u = jnp.where(t < 4, t, t - late_units)

        @pl.when((t >= 4) & (u == 4) & (s > 0))
        def _():
            for copy in halo:
                copy.wait_recv()

        @pl.when((t < 4) | ((u >= 4) & (u < 16)))
        def _():
            window_unit(u)

        c = t - late_relay

        @pl.when((c >= 0) & (c < NCH) & (s > 0))
        def _():
            remote(chunk(c), chunk(c), bs_send.at[c, 0], bs_recv.at[c], mate).wait_recv()
            chunk_sends(c, lambda copy: copy.start())

    def glob(slot, h):
        return gbuf[slot * 2 + h // 2, :, pl.ds(pl.multiple_of((h % 2) * HD, HD), HD)]

    @pl.loop(0, LH)
    def _(h):
        cols = pl.ds(pl.multiple_of(h * HD, HD), HD)
        loc = pl.ds(RIM, TOK)
        sc = mm_t(kc[loc, cols], glob(0, h)) * SCALE
        dp = mm_t(vc[loc, cols], glob(2, h))
        top = jnp.max(sc, axis=0, keepdims=True)
        ex = jnp.exp(sc - top)
        srt[h] = sc
        dpt[h] = dp
        st1[core, pl.ds(h, 1), :] = top
        st1[core, pl.ds(h + 4, 1), :] = jnp.sum(ex, axis=0, keepdims=True)
        st1[core, pl.ds(h + 8, 1), :] = jnp.sum(ex * dp, axis=0, keepdims=True)

    st1_copy = remote(st1.at[core], st1.at[core], s1_send.at[0], s1_recv.at[0], mate)
    st1_copy.start()

    def merge(ref, n):
        top = ref[0, 0:4, :]
        for i in range(1, n):
            top = jnp.maximum(top, ref[i, 0:4, :])
        tot = jnp.zeros((4, GLB), F32)
        dot = jnp.zeros((4, GLB), F32)
        for i in range(n):
            f = jnp.exp(ref[i, 0:4, :] - top)
            tot = tot + f * ref[i, 4:8, :]
            dot = dot + f * ref[i, 8:12, :]
        return top, tot, dot

    def put(ref, i, stats):
        for j, value in enumerate(stats):
            ref[i, j * 4:(j + 1) * 4, :] = value

    def lx_copies(b):
        rows = pl.ds(b * BLK, BLK)
        return [
            pltpu.make_async_remote_copy(
                src_ref=lp.at[(x + d) % NX, rows], dst_ref=lr.at[d - 1, rows],
                send_sem=lx_send.at[b, d - 1], recv_sem=lx_recv.at[b, d - 1],
                device_id={"head": (x + d) % NX}, device_id_type=MESH)
            for d in range(1, NX)
        ]

    def project(b):
        rows = pl.ds(b * BLK, BLK)
        for n in range(NX):
            lp[n, rows, :] = mm(attn_s[rows, :], w_s[:, n * COLS:(n + 1) * COLS]).astype(BF)
        for copy in lx_copies(b):
            copy.start()

    def forward(b):
        @pl.loop(0, LH)
        def _(h):
            rows, _, cols = spans(b, h)
            i = b * LH + h
            sg = mm_t(q_s[rows, cols], glob(1, h)) * SCALE
            top = jnp.maximum(mw[i], jnp.max(sg, axis=1, keepdims=True))
            eg = jnp.exp(sg - top)
            fac = jnp.exp(mw[i] - top)
            inv = 1.0 / (lw[i] * fac + jnp.sum(eg, axis=1, keepdims=True))
            out = (uw[rows, cols] * fac + mm(eg.astype(BF), glob(3, h))) * inv
            attn_s[rows, cols] = out.astype(BF)
            cw[i] = fac * inv
            pg_s[i] = eg * inv

        @pl.when(s > 0)
        def _():
            project(b)

    forward(0)
    st1_copy.wait()
    put(st2, y, merge(st1, 2))
    st2_copies = [
        remote(st2.at[y], st2.at[y], s2_send.at[d - 1], s2_recv.at[d - 1], seq_of((y + d) % NY, z, core))
        for d in range(1, NY)
    ]
    for copy in st2_copies:
        copy.start()
    forward(1)
    for d in range(1, NY):
        src = (y + NY - d) % NY
        remote(st2.at[src], st2.at[src], s2_send.at[d - 1], s2_recv.at[d - 1], mate).wait_recv()
    put(st3, z, merge(st2, NY))
    st3_copies = [
        remote(st3.at[z], st3.at[z], s3_send.at[d - 1], s3_recv.at[d - 1], seq_of(y, (z + d) % NZ, core))
        for d in range(1, NZ)
    ]
    for copy in st3_copies:
        copy.start()
    forward(2)
    forward(3)

    @pl.loop(0, NB * LH)
    def _(i):
        b = i // LH
        h = i % LH
        rows, _, cols = spans(b, h)
        da = da_s[rows, cols]
        delta = jnp.sum(da.astype(F32) * attn_s[rows, cols].astype(F32), axis=1, keepdims=True)
        pg = pg_s[i]
        ds = pg * (mm_t(da, glob(3, h)) - delta)
        dqa[rows, cols] = mm(ds.astype(BF), glob(1, h))
        dkg[:, cols] += mm(ds.T.astype(BF), q_s[rows, cols])
        dvg[:, cols] += mm(pg.T.astype(BF), da)

    def sib_copy(t):
        return remote(rb.at[t * 2 + 1 - core], sib.at[t], sib_send.at[t], sib_recv.at[t], mate)

    for t, part in ((2, dkg), (3, dvg)):
        for half in range(2):
            rb[t * 2 + half] = part[:, half * 256:(half + 1) * 256].astype(BF)
        sib_copy(t).start()

    for d in range(1, NZ):
        src = (z + NZ - d) % NZ
        remote(st3.at[src], st3.at[src], s3_send.at[d - 1], s3_recv.at[d - 1], mate).wait_recv()
    top, tot, dot = merge(st3, NZ)
    put(st1, core, (top + jnp.log(tot), dot / tot))

    @pl.loop(0, LH)
    def _(h):
        cols = pl.ds(pl.multiple_of(h * HD, HD), HD)
        loc = pl.ds(RIM, TOK)
        prob = jnp.exp(srt[h] - st1[core, pl.ds(h, 1), :])
        ds = prob * (dpt[h] - st1[core, pl.ds(h + 4, 1), :])
        half = h // 2
        lane = pl.ds(pl.multiple_of((h % 2) * HD, HD), HD)
        rb[half, :, lane] = mm(prob.T.astype(BF), vc[loc, cols]).astype(BF)
        rb[2 + half, :, lane] = mm(ds.T.astype(BF), kc[loc, cols]).astype(BF)
        dkc[loc, cols] += mm(ds.astype(BF), glob(0, h))
        dvc[loc, cols] += mm(prob.astype(BF), glob(2, h))

    for t in (0, 1):
        sib_copy(t).start()

    def rs_copies(t):
        copies = []
        for d in range(1, NZ):
            to = (z + d) % NZ
            copies.append(remote(
                comb.at[t, pl.ds(pl.multiple_of(to * 32, 32), 32), :], rs.at[t, d - 1],
                rs_send.at[t, d - 1], rs_recv.at[t, d - 1], seq_of(y, to, core)))
        return copies

    def reduce_pair(t):
        sib_copy(t).wait()
        comb[t] = (rb[t * 2 + core].astype(F32) + sib[t].astype(F32)).astype(BF)
        for copy in rs_copies(t):
            copy.start()

    def og_copy(t):
        return remote(sl.at[t], ogat.at[t, s], og_send.at[t], og_recv.at[t], 0)

    def reduce_line(t):
        for copy in rs_copies(t):
            copy.wait()
        total = comb[t, pl.ds(pl.multiple_of(z * 32, 32), 32), :].astype(F32)
        for d in range(NZ - 1):
            total = total + rs[t, d].astype(F32)
        sl[t] = total.astype(BF)

        @pl.when(s > 0)
        def _():
            og_copy(t).start()

        @pl.when(owner)
        def _():
            ogat[t, 0] = total.astype(BF)

    def window_back(b):
        @pl.loop(0, LH)
        def _(h):
            rows, win, cols = spans(b, h)
            i = b * LH + h
            da = da_s[rows, cols]
            delta = jnp.sum(da.astype(F32) * attn_s[rows, cols].astype(F32), axis=1, keepdims=True)
            prob = ew[i] * cw[i]
            ds = prob * (dpw[i] - delta)
            dqa[rows, cols] += mm(ds.astype(BF), kc[win, cols])
            dkc[win, cols] += mm(ds.T.astype(BF), q_s[rows, cols])
            dvc[win, cols] += mm(prob.T.astype(BF), da)

    for t in (2, 3):
        reduce_pair(t)
    window_back(0)
    for t in (0, 1):
        reduce_pair(t)
    window_back(1)
    window_back(2)
    back = [
        remote(hbs.at[i], hbr.at[i], hb_send_sem.at[i], hb_recv_sem.at[i], prv) for i in range(2)
    ]
    hbs[0] = dkc[pl.ds(0, RIM), :].astype(BF)
    hbs[1] = dvc[pl.ds(0, RIM), :].astype(BF)

    @pl.when(s > 0)
    def _():
        for copy in back:
            copy.start()

    for t in (2, 3, 0, 1):
        reduce_line(t)
    window_back(3)

    @pl.when(s < NS - 1)
    def _():
        for i, acc in enumerate((dkc, dvc)):
            back[i].wait_recv()
            acc[pl.ds(RIM + BLK, RIM), :] += hbr[i].astype(F32)

    @pl.when(owner)
    def _():
        for t in (2, 3, 0, 1):
            whole = ogat.at[t, pl.ds(1, NS - 1)]
            pltpu.make_async_copy(whole, whole, og_recv.at[t]).wait()
            for zz in range(NZ):
                for cc in range(2):
                    total = ogat[t, zz * 2 + cc].astype(F32)
                    for yy in range(1, NY):
                        total = total + ogat[t, yy * 16 + zz * 2 + cc].astype(F32)
                    rt[t, zz * 32:(zz + 1) * 32, cc * 256:(cc + 1) * 256] = total.astype(BF)
            if t == 0:
                is_col = jnp.max(oh_s[...].astype(F32), axis=1, keepdims=True)
                attn_s[...] = jnp.where(
                    is_col > 0, mm(oh_s[...], rt[0]), attn_s[...].astype(F32)).astype(BF)
                for b in range(NB):
                    project(b)
            else:
                acc, rows = ((dqa, pl.ds(0, TOK)), (dkc, pl.ds(RIM, TOK)), (dvc, pl.ds(RIM, TOK)))[t - 1]
                acc[rows, :] += mm(oh_s[...], rt[t])

    gq_out[...] = (dqa[...] * SCALE).astype(BF)
    gk_out[...] = (dkc[pl.ds(RIM, TOK), :] * SCALE).astype(BF)
    gv_out[...] = dvc[pl.ds(RIM, TOK), :].astype(BF)

    for b in range(NB):
        rows = pl.ds(b * BLK, BLK)
        for copy in lx_copies(b):
            copy.wait()
        total = lp[x, rows, :].astype(F32)
        for d in range(NX - 1):
            total = total + lr[d, rows, :].astype(F32)
        lo_out[rows, :] = total.astype(BF)

    @pl.loop(0, NCH)
    def _(c):
        chunk_sends(c, lambda copy: copy.wait_send())

    for copy in st2_copies + st3_copies:
        copy.wait_send()

    @pl.when(s < NS - 1)
    def _():
        for copy in halo:
            copy.wait_send()

    @pl.when(s > 0)
    def _():
        for copy in back:
            copy.wait_send()
        for t in range(4):
            og_copy(t).wait_send()


def vmem(*shape, dtype=F32):
    return pltpu.VMEM(shape, dtype)


def on_device(queries, keys, values, out_weight, out_grad, global_pos, block_mask):
    dma = pltpu.SemaphoreType.DMA
    out = jax.ShapeDtypeStruct((TOK, COLS), BF)
    any_spec = pl.BlockSpec(memory_space=pl.ANY)
    vm_spec = pl.BlockSpec(memory_space=pltpu.VMEM)
    scratch = [
        vmem(TOK, COLS, dtype=BF), vmem(RIM + TOK, COLS, dtype=BF), vmem(RIM + TOK, COLS, dtype=BF),
        vmem(COLS, D, dtype=BF), vmem(TOK, D, dtype=BF), vmem(TOK, COLS, dtype=BF),
        vmem(TOK, GLB, dtype=BF), vmem(8, GLB, 256, dtype=BF), vmem(NB, BLK, WBLK * BLK),
        vmem(16, BLK, 512), vmem(16, BLK, 512), vmem(16, BLK, 1), vmem(16, BLK, 1), vmem(16, BLK, 1),
        vmem(TOK, COLS), vmem(16, BLK, GLB), vmem(TOK, COLS, dtype=BF),
        vmem(NX, TOK, COLS, dtype=BF), vmem(NX - 1, TOK, COLS, dtype=BF),
        vmem(RIM + TOK, COLS), vmem(RIM + TOK, COLS), vmem(TOK, COLS), vmem(GLB, COLS), vmem(GLB, COLS),
        vmem(2, RIM, COLS, dtype=BF), vmem(2, RIM, COLS, dtype=BF),
        vmem(2, 16, GLB), vmem(NY, 16, GLB), vmem(NZ, 16, GLB), vmem(LH, TOK, GLB), vmem(LH, TOK, GLB),
        vmem(8, GLB, 256, dtype=BF), vmem(4, GLB, 256, dtype=BF), vmem(4, GLB, 256, dtype=BF),
        vmem(4, NZ - 1, 32, 256, dtype=BF), vmem(4, 32, 256, dtype=BF), vmem(4, NS, 32, 256, dtype=BF),
        vmem(4, GLB, COLS, dtype=BF),
        dma((5,)), dma((NCH, 5)), dma((NCH,)), dma((2,)), dma((2,)), dma((2,)), dma((2,)),
        dma((NB, NX - 1)), dma((NB, NX - 1)), dma((1,)), dma((1,)), dma((NY - 1,)), dma((NY - 1,)),
        dma((NZ - 1,)), dma((NZ - 1,)), dma((4,)), dma((4,)), dma((4, NZ - 1)), dma((4, NZ - 1)),
        dma((4,)), dma((4,)),
    ]
    return pl.pallas_call(
        kernel,
        out_shape=(out,) * 4,
        in_specs=[any_spec] * 5 + [vm_spec, pl.BlockSpec(memory_space=pltpu.SMEM)],
        out_specs=(vm_spec,) * 4,
        scratch_shapes=scratch,
        compiler_params=pltpu.CompilerParams(vmem_limit_bytes=64000000, has_side_effects=True),
    )(queries, keys, values, out_weight, out_grad, global_pos.reshape(1, GLB), block_mask)


def solution(mesh):
    return jax.shard_map(
        on_device,
        mesh=mesh,
        in_specs=(
            P("seq", "head"), P("seq", "head"), P("seq", "head"),
            P("head", None), P("seq", None), P(), P("seq", None),
        ),
        out_specs=(P("seq", "head"),) * 4,
        check_vma=False,
    )
```

time: 829 us -> 215 us (0.26); the launches traced: 817 us -> 215 us
  waiting for transfers between devices: 341 us -> 0 us
  blocking collectives: 250 us -> 0 us
  Pallas kernels: 0 us -> 209 us
  local copies, waits for them, and re-layouts: 99.9 us -> 5.42 us
  matrix products: 56.3 us -> 0 us
  other arithmetic: 38 us -> 0 us
  starting transfers between devices: 17.6 us -> 0 us
  between operations: 14.7 us -> 0.66 us
    psum x3 -> x0, waiting for transfers between devices: 325 us -> none  [the longest x1 152 us: spread(): return lax.psum(kept, axis)]
    pallas_call x0 -> x1, Pallas kernels: none -> 209 us  [on_device(): pl.pallas_call(kernel, out_shape=(out,) * 4, in_specs=[any_spec] * 5 + [v...]
    pmax x1 -> x0, blocking collectives: 126 us -> none  [on_device(): row_max = lax.pmax(jnp.max(row_scores, axis=2), 'seq')]
    psum x1 -> x0, blocking collectives: 124 us -> none  [on_device(): lax.psum((jnp.sum(row_exp, axis=2), jnp.einsum('hgt,thd->hgd', row_exp, v...]
    dot_general x21 -> x0, matrix products: 56.3 us -> none  [the longest x1 4.67 us: on_device(): jnp.einsum('bihd,brjhd->hbirj', dattn_blk, value_win, preferred_element_t...]
    another operation x17 -> x0, local copies, waits for them, and re-layouts: 23.4 us -> none  [the longest x13 16.6 us: window_stack(): jnp.stack([blocks[WBLK - 1 - offset:WBLK - 1 - offset + n_blocks] for off...]
    reshape x12 -> x0, local copies, waits for them, and re-layouts: 20.1 us -> none  [the longest x3 6.11 us: owner_rows(): summed.reshape(GLOBALS, local_cols)]
    scatter-add x9 -> x0, other arithmetic: 19 us -> none  [the longest x3 11 us: owner_rows(): placed = jnp.zeros((tok_rows, local_cols), jnp.float32).at[global_pos].ad...]
  transfers between devices with their start and end apart: 8 -> 0, of which waited for: 4 -> 0; matrix products, arithmetic and copies ran while one was open for 16% -> 0% of each run, Pallas kernels for 0% -> 0%
where the time goes in v1:
time: 215 us
  Pallas kernels  209 us (97%)
  local copies, waits for them, and re-layouts  5.42 us (3%)
    pallas_call x1, Pallas kernels, on_device(): pl.pallas_call(kernel, out_shape=(out,) * 4, in_specs=[any_spec] * 5 + [v...  209 us
    unnamed x8, local copies, waits for them, and re-layouts  5.42 us

profile of v1, /device:TPU:2, one launch (start us, length us, event | category | flops | bytes accessed | tf_op | source)
XLA Modules:
  0.0 214.6 jit_solution(8088604302795649758)
XLA Ops:
  0.6 208.6 %shard_map.102 = (bf16[512,512]{1,0:T(8,128)(2,1)}, bf16[512,512]{1,0:T(8,128)(2,1)}, bf16[512,512]{1,0:T(8,128)(2,1)}, bf16[512,512]{1,0:T(8,128)(2,1)}) custom-call(bf16[512,512]{1,0:T(8,128)(2,1)} %q_hbm.1, bf16[512,512]{1,0:T(8,128)(2,1)} %k_hbm.1, bf16[512,512]{1,0:T(8,128)(2,1)} %v_hbm.1, bf16[512,2048]{1,0:T(8,128)(2,1)} %w_hbm.1, ...), custom_call_target="tpu_custom_call" | custom-call | tf_op jit(solution)/shard_map/pallas_call | solution.py:533
  209.2 0.0 copy-start.1
  209.2 0.0 copy-start
  209.2 2.0 copy.15
  211.2 1.9 copy.16
  213.0 0.0 copy-done.1
  213.0 0.8 copy.17
  213.8 0.0 copy-done
  213.8 0.8 copy.18
Async XLA Ops:
  209.2 3.8 %copy-start.1 = (bf16[512,512]{1,0:T(8,128)(2,1)S(1)}, bf16[512,512]{1,0:T(8,128)(2,1)}, u32[]{:S(2)}) copy-start(bf16[512,512]{1,0:T(8,128)(2,1)} %get-tuple-element.10) | copy-start | bytes 1572868
  209.2 4.6 %copy-start = (bf16[512,512]{1,0:T(8,128)(2,1)S(1)}, bf16[512,512]{1,0:T(8,128)(2,1)}, u32[]{:S(2)}) copy-start(bf16[512,512]{1,0:T(8,128)(2,1)} %get-tuple-element.11) | copy-start | bytes 1572868

commit v2 on v1

--- a/solution.py
+++ b/solution.py
@@ -21,7 +21,7 @@
 NZ = 8
 NS = 64
 NX = 4
-NCH = 16
+NCH = 8
 SCALE = 1.0 / math.sqrt(HD)
 NEG = -1e30
 F32 = jnp.float32
@@ -116,26 +116,32 @@
     zp0, zm0, yp0, ym0 = tree(z, NZ, y, NY)
     yp1, ym1, zp1, zm1 = tree(y, NY, z, NZ)
     dirs = (
-        (zp0, zp1, seq_of(y, (z + 1) % NZ, 0)),
-        (zm0, zm1, seq_of(y, (z + NZ - 1) % NZ, 0)),
-        (yp0, yp1, seq_of((y + 1) % NY, z, 0)),
-        (ym0, ym1, seq_of((y + NY - 1) % NY, z, 0)),
+        (zp0, zp1, seq_of(y, (z + 1) % NZ, core)),
+        (zm0, zm1, seq_of(y, (z + NZ - 1) % NZ, core)),
+        (yp0, yp1, seq_of((y + 1) % NY, z, core)),
+        (ym0, ym1, seq_of((y + NY - 1) % NY, z, core)),
     )
 
-    def chunk(c):
-        start = pl.multiple_of(((c // 2) % 2) * 128, 128)
-        return gbuf.at[(c // 4) * 2 + c % 2, pl.ds(start, 128), :]
+    def chunk(c, half):
+        start = pl.multiple_of((c % 2) * 128, 128)
+        return gbuf.at[(c // 2) * 2 + half, pl.ds(start, 128), :]
+
+    def chunk_copy(c, half, d, dev):
+        return remote(chunk(c, half), chunk(c, half), bs_send.at[c, d], bs_recv.at[c, half], dev)
 
     def chunk_sends(c, act):
-        half = c % 2
         for d, (c0, c1, dev) in enumerate(dirs):
-            @pl.when((c0 * (1 - half) + c1 * half) * (1 - core) > 0)
+            @pl.when(c0 * (1 - core) + c1 * core > 0)
             def _():
-                act(remote(chunk(c), chunk(c), bs_send.at[c, d], bs_recv.at[c], dev))
-
-        @pl.when(core == 0)
-        def _():
-            act(remote(chunk(c), chunk(c), bs_send.at[c, 4], bs_recv.at[c], mate))
+                act(chunk_copy(c, core, d, dev))
+
+        @pl.when(owner)
+        def _():
+            act(chunk_copy(c, 1, 5, mate))
+
+        @pl.when(s != 1)
+        def _():
+            act(chunk_copy(c, core, 4, mate))
 
     def gather(slot, src):
         got = mm(oh_s[...].astype(F32).T.astype(BF), src).astype(BF)
@@ -143,7 +149,7 @@
         gbuf[slot * 2 + 1, :, :] = got[:, 256:]
 
     def send_chunks(first):
-        @pl.loop(first, first + 8)
+        @pl.loop(first, first + 4)
         def _(c):
             chunk_sends(c, lambda copy: copy.start())
 
@@ -165,7 +171,7 @@
     def _():
         gather(2, da_s[...])
         gather(3, vc[pl.ds(RIM, TOK), :])
-        send_chunks(8)
+        send_chunks(4)
         is_col = jnp.max(oh_s[...].astype(F32), axis=1, keepdims=True)
         da_s[...] = jnp.where(is_col > 0, 0.0, da_s[...].astype(F32)).astype(BF)
 
@@ -211,12 +217,12 @@
 
     dz = jnp.minimum(z, NZ - z)
     dy = jnp.minimum(y, NY - y)
-    depth = dz + dy
-    leaf = flag(depth > 5) + core
-    late_units = jnp.where(leaf > 0, 0, jnp.maximum(16 - 4 * depth, 0))
-    late_relay = jnp.where(leaf > 0, 16, jnp.where(depth == 5, 4, 0))
-
-    @pl.loop(0, 32)
+    turned = flag(core == 0) * flag(z == 0) * flag(y != 0) + flag(core == 1) * flag(y == 0) * flag(z != 0)
+    depth = dz + dy + 2 * turned
+    late_units = jnp.where(depth < 4, 4, 0)
+    late_relay = jnp.where(depth < 4, 0, jnp.where(depth == 4, 4, jnp.where(depth == 5, 8, 16)))
+
+    @pl.loop(0, 24)
     def _(t):
         u = jnp.where(t < 4, t, t - late_units)
 
@@ -233,8 +239,14 @@
 
         @pl.when((c >= 0) & (c < NCH) & (s > 0))
         def _():
-            remote(chunk(c), chunk(c), bs_send.at[c, 0], bs_recv.at[c], mate).wait_recv()
+            chunk_copy(c, core, 0, mate).wait_recv()
             chunk_sends(c, lambda copy: copy.start())
+
+    @pl.when(s > 0)
+    def _():
+        @pl.loop(0, NCH)
+        def _(c):
+            chunk_copy(c, 1 - core, 0, mate).wait_recv()
 
     def glob(slot, h):
         return gbuf[slot * 2 + h // 2, :, pl.ds(pl.multiple_of((h % 2) * HD, HD), HD)]
@@ -341,8 +353,8 @@
         pg = pg_s[i]
         ds = pg * (mm_t(da, glob(3, h)) - delta)
         dqa[rows, cols] = mm(ds.astype(BF), glob(1, h))
-        dkg[:, cols] += mm(ds.T.astype(BF), q_s[rows, cols])
-        dvg[:, cols] += mm(pg.T.astype(BF), da)
+        dkg[:, cols] += mm(ds.astype(BF).T, q_s[rows, cols])
+        dvg[:, cols] += mm(pg.astype(BF).T, da)
 
     def sib_copy(t):
         return remote(rb.at[t * 2 + 1 - core], sib.at[t], sib_send.at[t], sib_recv.at[t], mate)
@@ -366,8 +378,8 @@
         ds = prob * (dpt[h] - st1[core, pl.ds(h + 4, 1), :])
         half = h // 2
         lane = pl.ds(pl.multiple_of((h % 2) * HD, HD), HD)
-        rb[half, :, lane] = mm(prob.T.astype(BF), vc[loc, cols]).astype(BF)
-        rb[2 + half, :, lane] = mm(ds.T.astype(BF), kc[loc, cols]).astype(BF)
+        rb[half, :, lane] = mm(prob.astype(BF).T, vc[loc, cols]).astype(BF)
+        rb[2 + half, :, lane] = mm(ds.astype(BF).T, kc[loc, cols]).astype(BF)
         dkc[loc, cols] += mm(ds.astype(BF), glob(0, h))
         dvc[loc, cols] += mm(prob.astype(BF), glob(2, h))
 
@@ -418,8 +430,8 @@
             prob = ew[i] * cw[i]
             ds = prob * (dpw[i] - delta)
             dqa[rows, cols] += mm(ds.astype(BF), kc[win, cols])
-            dkc[win, cols] += mm(ds.T.astype(BF), q_s[rows, cols])
-            dvc[win, cols] += mm(prob.T.astype(BF), da)
+            dkc[win, cols] += mm(ds.astype(BF).T, q_s[rows, cols])
+            dvc[win, cols] += mm(prob.astype(BF).T, da)
 
     for t in (2, 3):
         reduce_pair(t)
@@ -503,6 +515,11 @@
             og_copy(t).wait_send()
 
 
+def hand_over(*refs):
+    for src, dst in zip(refs[:4], refs[4:]):
+        dst[...] = src[...]
+
+
 def vmem(*shape, dtype=F32):
     return pltpu.VMEM(shape, dtype)
 
@@ -525,12 +542,12 @@
         vmem(8, GLB, 256, dtype=BF), vmem(4, GLB, 256, dtype=BF), vmem(4, GLB, 256, dtype=BF),
         vmem(4, NZ - 1, 32, 256, dtype=BF), vmem(4, 32, 256, dtype=BF), vmem(4, NS, 32, 256, dtype=BF),
         vmem(4, GLB, COLS, dtype=BF),
-        dma((5,)), dma((NCH, 5)), dma((NCH,)), dma((2,)), dma((2,)), dma((2,)), dma((2,)),
+        dma((5,)), dma((NCH, 6)), dma((NCH, 2)), dma((2,)), dma((2,)), dma((2,)), dma((2,)),
         dma((NB, NX - 1)), dma((NB, NX - 1)), dma((1,)), dma((1,)), dma((NY - 1,)), dma((NY - 1,)),
         dma((NZ - 1,)), dma((NZ - 1,)), dma((4,)), dma((4,)), dma((4, NZ - 1)), dma((4, NZ - 1)),
         dma((4,)), dma((4,)),
     ]
-    return pl.pallas_call(
+    outs = pl.pallas_call(
         kernel,
         out_shape=(out,) * 4,
         in_specs=[any_spec] * 5 + [vm_spec, pl.BlockSpec(memory_space=pltpu.SMEM)],
@@ -538,6 +555,14 @@
         scratch_shapes=scratch,
         compiler_params=pltpu.CompilerParams(vmem_limit_bytes=64000000, has_side_effects=True),
     )(queries, keys, values, out_weight, out_grad, global_pos.reshape(1, GLB), block_mask)
+    tile = pl.BlockSpec((BLK, COLS), lambda i: (i, 0))
+    return pl.pallas_call(
+        hand_over,
+        grid=(TOK // BLK,),
+        out_shape=(out,) * 4,
+        in_specs=[tile] * 4,
+        out_specs=(tile,) * 4,
+    )(*outs)
 
 
 def solution(mesh):

time: 215 us -> 124 us (0.58)
  Pallas kernels: 209 us -> 123 us
  local copies, waits for them, and re-layouts: 5.42 us -> 0 us
    pallas_call x1, Pallas kernels: 209 us -> 119 us  [on_device(): pl.pallas_call(kernel, out_shape=(out,) * 4, in_specs=[any_spec] * 5 + [v...]
    unnamed x8 -> x0, local copies, waits for them, and re-layouts: 5.42 us -> none
    pallas_call x0 -> x1, Pallas kernels: none -> 3.81 us  [on_device(): pl.pallas_call(hand_over, grid=(TOK // BLK,), out_shape=(out,) * 4, in_sp...]
where the time goes in v2:
time: 124 us
  Pallas kernels  123 us (99%)
    pallas_call x1, Pallas kernels, on_device(): pl.pallas_call(kernel, out_shape=(out,) * 4, in_specs=[any_spec] * 5 + [v...  119 us
    pallas_call x1, Pallas kernels, on_device(): pl.pallas_call(hand_over, grid=(TOK // BLK,), out_shape=(out,) * 4, in_sp...  3.81 us

profile of v2, /device:TPU:2, one launch (start us, length us, event | category | flops | bytes accessed | tf_op | source)
XLA Modules:
  0.0 123.9 jit_solution(5768465361998448429)
XLA Ops:
  0.6 119.4 %shard_map.102 = (bf16[512,512]{1,0:T(8,128)(2,1)}, bf16[512,512]{1,0:T(8,128)(2,1)}, bf16[512,512]{1,0:T(8,128)(2,1)}, bf16[512,512]{1,0:T(8,128)(2,1)}) custom-call(bf16[512,512]{1,0:T(8,128)(2,1)} %q_hbm.1, bf16[512,512]{1,0:T(8,128)(2,1)} %k_hbm.1, bf16[512,512]{1,0:T(8,128)(2,1)} %v_hbm.1, bf16[512,2048]{1,0:T(8,128)(2,1)} %w_hbm.1, ...), custom_call_target="tpu_custom_call" | custom-call | tf_op jit(solution)/shard_map/pallas_call | solution.py:550
  120.0 3.8 %shard_map.103 = (bf16[512,512]{1,0:T(8,128)(2,1)}, bf16[512,512]{1,0:T(8,128)(2,1)}, bf16[512,512]{1,0:T(8,128)(2,1)}, bf16[512,512]{1,0:T(8,128)(2,1)}) custom-call(bf16[512,512]{1,0:T(8,128)(2,1)} %get-tuple-element.8.refs_0_, bf16[512,512]{1,0:T(8,128)(2,1)} %get-tuple-element.9.refs_1_, bf16[512,512]{1,0:T(8,128)(2,1)} %get-tuple-element.10.refs_2_, ...), custom_call_target="tpu_custom_call" | custom-call | tf_op jit(solution)/shard_map/pallas_call | solution.py:559

commit v3 on v2

--- a/solution.py
+++ b/solution.py
@@ -44,14 +44,14 @@
 def kernel(
     q_hbm, k_hbm, v_hbm, w_hbm, og_hbm, gpos, bmask,
     lo_out, gq_out, gk_out, gv_out,
-    q_s, kc, vc, w_s, og_s, da_s, oh_s, gbuf, bias,
+    q_s, kc, vc, w_s, og_s, da_s, oh_s, keep, gbuf, bias,
     ew, dpw, mw, lw, cw, uw, pg_s, attn_s,
     lp, lr, dkc, dvc, dqa, dkg, dvg, hbs, hbr,
     st1, st2, st3, srt, dpt,
-    rb, sib, comb, rs, sl, ogat, rt,
+    rb, sib, comb, rs, sl, own, yr, ol, rt, lpr, lrr,
     ld_sem, bs_send, bs_recv, halo_send, halo_recv, hb_send_sem, hb_recv_sem,
     lx_send, lx_recv, s1_send, s1_recv, s2_send, s2_recv, s3_send, s3_recv,
-    sib_send, sib_recv, rs_send, rs_recv, og_send, og_recv,
+    sib_send, sib_recv, rs_send, rs_recv, yr_send, yr_recv, og_send, og_recv, lr_send, lr_recv,
 ):
     s = lax.axis_index("seq")
     x = lax.axis_index("head")
@@ -105,6 +105,7 @@
     own_f = jnp.where(owner, 1.0, 0.0).astype(F32)
     one_f = jnp.where(s == 1, 1.0, 0.0).astype(F32)
     oh_s[...] = (hits * own_f).astype(BF)
+    keep[...] = 1.0 - jnp.max(hits, axis=1, keepdims=True) * own_f
 
     def tree(a, na, b, nb):
         ap = flag(b == 0) * flag(a < na // 2)
@@ -172,8 +173,7 @@
         gather(2, da_s[...])
         gather(3, vc[pl.ds(RIM, TOK), :])
         send_chunks(4)
-        is_col = jnp.max(oh_s[...].astype(F32), axis=1, keepdims=True)
-        da_s[...] = jnp.where(is_col > 0, 0.0, da_s[...].astype(F32)).astype(BF)
+        da_s[...] = jnp.where(keep[...] > 0, da_s[...].astype(F32), 0.0).astype(BF)
 
     f_rim = is_row[:, 128:512] * one_f
     f_loc = is_row * own_f
@@ -312,13 +312,11 @@
             fac = jnp.exp(mw[i] - top)
             inv = 1.0 / (lw[i] * fac + jnp.sum(eg, axis=1, keepdims=True))
             out = (uw[rows, cols] * fac + mm(eg.astype(BF), glob(3, h))) * inv
-            attn_s[rows, cols] = out.astype(BF)
+            attn_s[rows, cols] = (out * keep[rows, :]).astype(BF)
             cw[i] = fac * inv
             pg_s[i] = eg * inv
 
-        @pl.when(s > 0)
-        def _():
-            project(b)
+        project(b)
 
     forward(0)
     st1_copy.wait()
@@ -343,8 +341,7 @@
     forward(2)
     forward(3)
 
-    @pl.loop(0, NB * LH)
-    def _(i):
+    def glob_back(i):
         b = i // LH
         h = i % LH
         rows, _, cols = spans(b, h)
@@ -358,11 +355,6 @@
 
     def sib_copy(t):
         return remote(rb.at[t * 2 + 1 - core], sib.at[t], sib_send.at[t], sib_recv.at[t], mate)
-
-    for t, part in ((2, dkg), (3, dvg)):
-        for half in range(2):
-            rb[t * 2 + half] = part[:, half * 256:(half + 1) * 256].astype(BF)
-        sib_copy(t).start()
 
     for d in range(1, NZ):
         src = (z + NZ - d) % NZ
@@ -401,8 +393,12 @@
         for copy in rs_copies(t):
             copy.start()
 
-    def og_copy(t):
-        return remote(sl.at[t], ogat.at[t, s], og_send.at[t], og_recv.at[t], 0)
+    def yr_copy(t, d):
+        return remote(sl.at[t], yr.at[t, d - 1], yr_send.at[t], yr_recv.at[t, d - 1], seq_of(0, z, core))
+
+    def og_copy(t, i):
+        place = rt.at[t, pl.ds(pl.multiple_of((i // 2) * 32, 32), 32), pl.ds(pl.multiple_of((i % 2) * 256, 256), 256)]
+        return remote(ol.at[t], place, og_send.at[t], og_recv.at[t, i], 0)
 
     def reduce_line(t):
         for copy in rs_copies(t):
@@ -410,15 +406,32 @@
         total = comb[t, pl.ds(pl.multiple_of(z * 32, 32), 32), :].astype(F32)
         for d in range(NZ - 1):
             total = total + rs[t, d].astype(F32)
-        sl[t] = total.astype(BF)
-
-        @pl.when(s > 0)
-        def _():
-            og_copy(t).start()
-
-        @pl.when(owner)
-        def _():
-            ogat[t, 0] = total.astype(BF)
+
+        @pl.when(y > 0)
+        def _():
+            sl[t] = total.astype(BF)
+            yr_copy(t, y).start()
+
+        @pl.when(y == 0)
+        def _():
+            own[t] = total
+
+    def reduce_column(t):
+        @pl.when(y == 0)
+        def _():
+            total = own[t]
+            for d in range(1, NY):
+                yr_copy(t, d).wait_recv()
+                total = total + yr[t, d - 1].astype(F32)
+
+            @pl.when(s > 0)
+            def _():
+                ol[t] = total.astype(BF)
+                og_copy(t, s).start()
+
+            @pl.when(owner)
+            def _():
+                rt[t, 0:32, 0:256] = total.astype(BF)
 
     def window_back(b):
         @pl.loop(0, LH)
@@ -433,12 +446,27 @@
             dkc[win, cols] += mm(ds.astype(BF).T, q_s[rows, cols])
             dvc[win, cols] += mm(prob.astype(BF).T, da)
 
+    @pl.loop(0, 8)
+    def _(i):
+        glob_back(i)
+
+    for t in (0, 1):
+        reduce_pair(t)
+
+    @pl.loop(8, 16)
+    def _(i):
+        glob_back(i)
+
+    for t, part in ((2, dkg), (3, dvg)):
+        for half in range(2):
+            rb[t * 2 + half] = part[:, half * 256:(half + 1) * 256].astype(BF)
+        sib_copy(t).start()
+    window_back(0)
+    window_back(1)
+    for t in (0, 1):
+        reduce_line(t)
     for t in (2, 3):
         reduce_pair(t)
-    window_back(0)
-    for t in (0, 1):
-        reduce_pair(t)
-    window_back(1)
     window_back(2)
     back = [
         remote(hbs.at[i], hbr.at[i], hb_send_sem.at[i], hb_recv_sem.at[i], prv) for i in range(2)
@@ -451,36 +479,41 @@
         for copy in back:
             copy.start()
 
-    for t in (2, 3, 0, 1):
+    for t in (0, 1):
+        reduce_column(t)
+    window_back(3)
+    for t in (2, 3):
         reduce_line(t)
-    window_back(3)
+    for t in (2, 3):
+        reduce_column(t)
+
+    def rows_here(t):
+        for i in range(1, 2 * NZ):
+            og_copy(t, i).wait_recv()
+
+    def lo_rows(d):
+        return pltpu.make_async_remote_copy(
+            src_ref=lpr.at[(x + d) % NX], dst_ref=lrr.at[d - 1],
+            send_sem=lr_send.at[d - 1], recv_sem=lr_recv.at[d - 1],
+            device_id={"head": (x + d) % NX}, device_id_type=MESH)
+
+    @pl.when(owner)
+    def _():
+        rows_here(0)
+        for d in (2, 1, 3, 0):
+            to = (x + d) % NX
+            lpr[to] = mm(rt[0], w_s[:, pl.ds(pl.multiple_of(to * COLS, COLS), COLS)]).astype(BF)
+            if d:
+                lo_rows(d).start()
+        for t, acc, rows in ((1, dqa, pl.ds(0, TOK)), (2, dkc, pl.ds(RIM, TOK)), (3, dvc, pl.ds(RIM, TOK))):
+            rows_here(t)
+            acc[rows, :] += mm(oh_s[...], rt[t])
 
     @pl.when(s < NS - 1)
     def _():
         for i, acc in enumerate((dkc, dvc)):
             back[i].wait_recv()
             acc[pl.ds(RIM + BLK, RIM), :] += hbr[i].astype(F32)
-
-    @pl.when(owner)
-    def _():
-        for t in (2, 3, 0, 1):
-            whole = ogat.at[t, pl.ds(1, NS - 1)]
-            pltpu.make_async_copy(whole, whole, og_recv.at[t]).wait()
-            for zz in range(NZ):
-                for cc in range(2):
-                    total = ogat[t, zz * 2 + cc].astype(F32)
-                    for yy in range(1, NY):
-                        total = total + ogat[t, yy * 16 + zz * 2 + cc].astype(F32)
-                    rt[t, zz * 32:(zz + 1) * 32, cc * 256:(cc + 1) * 256] = total.astype(BF)
-            if t == 0:
-                is_col = jnp.max(oh_s[...].astype(F32), axis=1, keepdims=True)
-                attn_s[...] = jnp.where(
-                    is_col > 0, mm(oh_s[...], rt[0]), attn_s[...].astype(F32)).astype(BF)
-                for b in range(NB):
-                    project(b)
-            else:
-                acc, rows = ((dqa, pl.ds(0, TOK)), (dkc, pl.ds(RIM, TOK)), (dvc, pl.ds(RIM, TOK)))[t - 1]
-                acc[rows, :] += mm(oh_s[...], rt[t])
 
     gq_out[...] = (dqa[...] * SCALE).astype(BF)
     gk_out[...] = (dkc[pl.ds(RIM, TOK), :] * SCALE).astype(BF)
@@ -495,6 +528,15 @@
             total = total + lr[d, rows, :].astype(F32)
         lo_out[rows, :] = total.astype(BF)
 
+    @pl.when(owner)
+    def _():
+        total = lpr[x].astype(F32)
+        for d in range(1, NX):
+            lo_rows(d).wait()
+            total = total + lrr[d - 1].astype(F32)
+        placed = mm(oh_s[...], total.astype(BF))
+        lo_out[...] = (lo_out[...].astype(F32) + placed).astype(BF)
+
     @pl.loop(0, NCH)
     def _(c):
         chunk_sends(c, lambda copy: copy.wait_send())
@@ -511,8 +553,16 @@
     def _():
         for copy in back:
             copy.wait_send()
+
+    @pl.when(y > 0)
+    def _():
         for t in range(4):
-            og_copy(t).wait_send()
+            yr_copy(t, y).wait_send()
+
+    @pl.when((y == 0) & (s > 0))
+    def _():
+        for t in range(4):
+            og_copy(t, s).wait_send()
 
 
 def hand_over(*refs):
@@ -532,7 +582,7 @@
     scratch = [
         vmem(TOK, COLS, dtype=BF), vmem(RIM + TOK, COLS, dtype=BF), vmem(RIM + TOK, COLS, dtype=BF),
         vmem(COLS, D, dtype=BF), vmem(TOK, D, dtype=BF), vmem(TOK, COLS, dtype=BF),
-        vmem(TOK, GLB, dtype=BF), vmem(8, GLB, 256, dtype=BF), vmem(NB, BLK, WBLK * BLK),
+        vmem(TOK, GLB, dtype=BF), vmem(TOK, 1), vmem(8, GLB, 256, dtype=BF), vmem(NB, BLK, WBLK * BLK),
         vmem(16, BLK, 512), vmem(16, BLK, 512), vmem(16, BLK, 1), vmem(16, BLK, 1), vmem(16, BLK, 1),
         vmem(TOK, COLS), vmem(16, BLK, GLB), vmem(TOK, COLS, dtype=BF),
         vmem(NX, TOK, COLS, dtype=BF), vmem(NX - 1, TOK, COLS, dtype=BF),
@@ -540,12 +590,13 @@
         vmem(2, RIM, COLS, dtype=BF), vmem(2, RIM, COLS, dtype=BF),
         vmem(2, 16, GLB), vmem(NY, 16, GLB), vmem(NZ, 16, GLB), vmem(LH, TOK, GLB), vmem(LH, TOK, GLB),
         vmem(8, GLB, 256, dtype=BF), vmem(4, GLB, 256, dtype=BF), vmem(4, GLB, 256, dtype=BF),
-        vmem(4, NZ - 1, 32, 256, dtype=BF), vmem(4, 32, 256, dtype=BF), vmem(4, NS, 32, 256, dtype=BF),
-        vmem(4, GLB, COLS, dtype=BF),
+        vmem(4, NZ - 1, 32, 256, dtype=BF), vmem(4, 32, 256, dtype=BF), vmem(4, 32, 256),
+        vmem(4, NY - 1, 32, 256, dtype=BF), vmem(4, 32, 256, dtype=BF),
+        vmem(4, GLB, COLS, dtype=BF), vmem(NX, GLB, COLS, dtype=BF), vmem(NX - 1, GLB, COLS, dtype=BF),
         dma((5,)), dma((NCH, 6)), dma((NCH, 2)), dma((2,)), dma((2,)), dma((2,)), dma((2,)),
         dma((NB, NX - 1)), dma((NB, NX - 1)), dma((1,)), dma((1,)), dma((NY - 1,)), dma((NY - 1,)),
         dma((NZ - 1,)), dma((NZ - 1,)), dma((4,)), dma((4,)), dma((4, NZ - 1)), dma((4, NZ - 1)),
-        dma((4,)), dma((4,)),
+        dma((4,)), dma((4, NY - 1)), dma((4,)), dma((4, 2 * NZ)), dma((NX - 1,)), dma((NX - 1,)),
     ]
     outs = pl.pallas_call(
         kernel,

time: 124 us -> 110 us (0.89)
  Pallas kernels: 123 us -> 109 us
    pallas_call x1, Pallas kernels: 119 us -> 105 us  [on_device(): pl.pallas_call(kernel, out_shape=(out,) * 4, in_specs=[any_spec] * 5 + [v...]
where the time goes in v3:
time: 110 us
  Pallas kernels  109 us (99%)
    pallas_call x1, Pallas kernels, on_device(): pl.pallas_call(kernel, out_shape=(out,) * 4, in_specs=[any_spec] * 5 + [v...  105 us
    pallas_call x1, Pallas kernels, on_device(): pl.pallas_call(hand_over, grid=(TOK // BLK,), out_shape=(out,) * 4, in_sp...  3.81 us

profile of v3, /device:TPU:2, one launch (start us, length us, event | category | flops | bytes accessed | tf_op | source)
XLA Modules:
  0.0 109.7 jit_solution(14648605258365307493)
XLA Ops:
  0.6 105.3 %shard_map.102 = (bf16[512,512]{1,0:T(8,128)(2,1)}, bf16[512,512]{1,0:T(8,128)(2,1)}, bf16[512,512]{1,0:T(8,128)(2,1)}, bf16[512,512]{1,0:T(8,128)(2,1)}) custom-call(bf16[512,512]{1,0:T(8,128)(2,1)} %q_hbm.1, bf16[512,512]{1,0:T(8,128)(2,1)} %k_hbm.1, bf16[512,512]{1,0:T(8,128)(2,1)} %v_hbm.1, bf16[512,2048]{1,0:T(8,128)(2,1)} %w_hbm.1, ...), custom_call_target="tpu_custom_call" | custom-call | tf_op jit(solution)/shard_map/pallas_call | solution.py:601
  105.9 3.8 %shard_map.103 = (bf16[512,512]{1,0:T(8,128)(2,1)}, bf16[512,512]{1,0:T(8,128)(2,1)}, bf16[512,512]{1,0:T(8,128)(2,1)}, bf16[512,512]{1,0:T(8,128)(2,1)}) custom-call(bf16[512,512]{1,0:T(8,128)(2,1)} %get-tuple-element.8.refs_0_, bf16[512,512]{1,0:T(8,128)(2,1)} %get-tuple-element.9.refs_1_, bf16[512,512]{1,0:T(8,128)(2,1)} %get-tuple-element.10.refs_2_, ...), custom_call_target="tpu_custom_call" | custom-call | tf_op jit(solution)/shard_map/pallas_call | solution.py:610
